TPU v7x, 512 devices: a whole 4x4x16 slice. The times are simulated.
512 devices in a mesh: dp: 16 (over z), tensor: 32 (over x, y, core).
Axes of the slice: x: 4, y: 4, z: 16, core: 2. Of those that a mesh axis runs over, the one named last changes fastest.
Arguments:
- hidden: bfloat16 [14336, 4096], P('dp', 'tensor')
- gain: bfloat16 [4096], P('tensor'), may hold values from 0.5 to 1.5
- head_weight: bfloat16 [4096, 32000], P('dp', 'tensor')
- targets: int32 [14336], P('dp'), may hold values from 0 to 31999
- seq_ids: int32 [14336], P(('dp', 'tensor')), may hold values from 0 to 63, never falling along the last dimension, each value on 1 to 1792 neighbouring positions
- live: int32 [14336], P(('dp', 'tensor')), may hold values 0 or 1
Outputs:
- logprob: float32 [14336], P(('dp', 'tensor'))
- entropy: float32 [14336], P(('dp', 'tensor'))
- seq_mean: float32 [64], replicated
Inputs may be any that keep to these rules, and one draw needn't show every extreme that they name: `seq_ids`: sequence numbers never fall along the tokens; each sequence has 1 to 1792 tokens, one exactly 1792.
All inputs are finite; a program needn't handle non-finite values. No bound on the sum of `live` on one device may be relied on, other than what follows from the above.
Results may differ from a plain program's by a relative error of at most 0.0015.
Values may be sent and summed in bfloat16 or wider, within the bound.
No kernel may reach another device: no remote copies, remote signals or barrier semaphores. Data moves between devices by JAX's collectives and lax.ppermute only.
A program may use at most 64 MiB of HBM per device.

v0:
```python
import jax
import jax.numpy as jnp
from jax import lax
from jax.sharding import PartitionSpec as P

SEQ_DEV = 4


def body(hidden, gain, head_weight, targets, seq_ids, live):
    shards = lax.axis_size("tensor")
    rank = lax.axis_index("tensor")
    tok_rows = hidden.shape[0]
    share = tok_rows // shards
    vocab_dev = head_weight.shape[1]
    whole, gains = (
        lax.all_gather(hidden, "tensor", axis=1, tiled=True),
        lax.all_gather(gain, "tensor", axis=0, tiled=True),
    )
    values = whole.astype(jnp.float32)
    meansq = jnp.mean(values * values, axis=-1, keepdims=True)
    normed = (values * lax.rsqrt(meansq + 1e-05) * gains.astype(jnp.float32)).astype(jnp.bfloat16)
    scores = jnp.dot(
        normed,
        lax.all_gather(head_weight, "dp", axis=0, tiled=True),
        preferred_element_type=jnp.float32,
    )
    top = jnp.max(scores, axis=-1)
    shifted = scores - top[:, None]
    expo = jnp.exp(shifted)
    total = jnp.sum(expo, axis=-1)
    spread = jnp.sum(expo * shifted, axis=-1)
    local_ids = targets - rank * vocab_dev
    inside = (local_ids >= 0) & (local_ids < vocab_dev)
    picked = jnp.take_along_axis(scores, jnp.clip(local_ids, 0, vocab_dev - 1)[:, None], axis=1)[
        :, 0
    ]
    target_score = jnp.where(inside, picked, 0.0)
    offset = rank * share
    best = lax.pmax(top, "tensor")
    scale = jnp.exp(top - best)
    sums = lax.psum(
        (total * scale, (spread + (top - best) * total) * scale, target_score), "tensor"
    )
    g_top = lax.dynamic_slice_in_dim(best, offset, share, 0)
    g_total = lax.dynamic_slice_in_dim(sums[0], offset, share, 0)
    g_spread = lax.dynamic_slice_in_dim(sums[1], offset, share, 0)
    g_target = lax.dynamic_slice_in_dim(sums[2], offset, share, 0)
    weight = live.astype(jnp.float32)
    log_total = jnp.log(g_total)
    logprob = (g_target - g_top - log_total) * weight
    entropy = (log_total - g_spread / g_total) * weight
    seq_count = SEQ_DEV * lax.axis_size("dp")
    member = (seq_ids[:, None] == jnp.arange(seq_count)[None, :]).astype(jnp.float32)
    seq_sums = jnp.sum(member * logprob[:, None], axis=0)
    seq_live = jnp.sum(member * weight[:, None], axis=0)
    seq_sums, seq_live = lax.psum((seq_sums, seq_live), ("dp", "tensor"))
    seq_mean = seq_sums / jnp.maximum(seq_live, 1.0)
    return (logprob, entropy, seq_mean)


def solution(mesh):
    placed = (
        P("dp", "tensor"),
        P("tensor"),
        P("dp", "tensor"),
        P("dp"),
        P(("dp", "tensor")),
        P(("dp", "tensor")),
    )
    return jax.shard_map(
        body,
        mesh=mesh,
        in_specs=placed,
        out_specs=(P(("dp", "tensor")), P(("dp", "tensor")), P()),
        check_vma=False,
    )
```

profile of v0, /device:TPU:1, one launch (start us, length us, event | category | flops | bytes accessed | tf_op | source)
XLA Modules:
  0.0 559.9 jit_solution(8000703077066795527)
XLA Ops:
  7.2 0.0 all-gather.4.cloned.1.call-start
  7.2 0.7 all-gather.4.cloned.1.call-update
  7.9 0.0 all-gather.6.cloned.1.call-start
  7.9 0.7 all-gather.6.cloned.1.call-update
  8.7 24.1 %all-gather = bf16[32,1,128]{2,1,0:T(2,128)(2,1)S(1)} all-gather(bf16[1,1,128]{2,1,0:T(2,128)(2,1)} %bitcast.6), channel_id=1, replica_groups=mesh['dp'=16,'tensor'=32] {'tensor'}, dimensions={0}, use_global_device_ids=true | all-gather | bytes 8448 | tf_op jit(solution)/shard_map/all_gather | solution.py:17
  32.8 0.7 compare_select_fusion
  33.5 0.7 convert_element_type.16
  34.2 54.0 %all-gather.4.cloned.1.call-done = bf16[896,4096]{1,0:T(8,128)(2,1)} async-done(((bf16[896,128]{1,0:T(8,128)(2,1)}), bf16[896,4096]{1,0:T(8,128)(2,1)}) %all-gather.4.cloned.1.call-update) | async-done | bytes 7340048 | tf_op jit(solution)/shard_map/all_gather | solution.py:16
  88.3 4.6 fusion
  92.8 114.5 %all-gather.6.cloned.1.call-done = bf16[4096,1000]{0,1:T(8,128)(2,1)} async-done(((bf16[256,1000]{0,1:T(8,128)(2,1)}), bf16[4096,1000]{0,1:T(8,128)(2,1)}) %all-gather.6.cloned.1.call-update) | async-done | bytes 8192016 | tf_op jit(solution)/shard_map/all_gather | solution.py:24
  207.3 14.7 %fusion.12 = (f32[896]{0:T(1024)S(1)}, f32[896,1000]{0,1:T(8,128)}) fusion(bf16[4096,1000]{0,1:T(8,128)(2,1)} %all-gather.6.cloned.1.call-done, bf16[896,4096]{1,0:T(8,128)(2,1)} %all-gather.4.cloned.1.call-done, f32[4096]{0:T(1024)S(1)} %bitcast.5, f32[896]{0:T(1024)S(1)} %add_rsqrt_fusion), kind=kOutput, calls=%fused_computation.30 | convolution fusion | flops 7355607040 | bytes 19139584 | tf_op jit(solution)/shard_map/dot_general | solution.py:22
  222.1 0.0 copy-start
  222.1 0.0 copy-start.3
  222.1 0.0 copy-start.2
  222.1 73.2 %pmax.7 = f32[896]{0:T(1024)S(1)} all-reduce(f32[896]{0:T(1024)S(1)} %get-tuple-element.16), channel_id=1, replica_groups=mesh['dp'=16,'tensor'=32] {'tensor'}, use_global_device_ids=true, to_apply=%region_3.0 | all-reduce | flops 896 | bytes 7168 | tf_op jit(solution)/shard_map/pmax | solution.py:39
  295.2 2.7 fusion.7
  298.0 30.1 %gather_fusion = f32[896]{0:T(1024)S(1)} fusion(f32[896,1000]{0,1:T(8,128)} %get-tuple-element.17, s32[896]{0:T(1024)S(1)} %fusion.11), kind=kCustom, calls=%fused_computation | custom fusion | bytes 14336 | tf_op jit(solution)/shard_map/jit(take_along_axis)/gather | solution.py:34
  328.1 0.0 copy-done
  328.2 121.3 %all-reduce.1 = (f32[896]{0:T(1024)S(1)}, f32[896]{0:T(1024)S(1)}, f32[896]{0:T(1024)S(1)}) all-reduce(f32[896]{0:T(1024)S(1)} %select_select_fusion, f32[896]{0:T(1024)S(1)} %get-tuple-element.13, f32[896]{0:T(1024)S(1)} %get-tuple-element.12), channel_id=1, replica_groups=mesh['dp'=16,'tensor'=32] {'tensor'}, use_global_device_ids=true, to_apply=%region_1.0 | all-reduce | flops 2688 | bytes 21504 | tf_op jit(solution)/shard_map/psum | solution.py:41
  449.4 0.0 copy-done.3
  449.4 0.6 subtract_multiply_fusion
  450.0 0.0 copy-start.1
  450.0 0.0 copy-done.2
  450.0 0.1 select_reduce_fusion
  450.1 102.4 %all-reduce = (f32[64]{0:T(128)S(1)}, f32[64]{0:T(128)S(1)}) all-reduce(f32[64]{0:T(128)S(1)} %get-tuple-element.6, f32[64]{0:T(128)S(1)} %get-tuple-element.5), channel_id=1, replica_groups=mesh['dp'=16,'tensor'=32] {'dp','tensor'}, use_global_device_ids=true, to_apply=%region_9.10 | all-reduce | flops 128 | bytes 1024 | tf_op jit(solution)/shard_map/psum | solution.py:56
  552.5 0.5 maximum_divide_fusion
  553.1 0.0 copy-done.1
  (8 shorter events, 0.1 us)
Async XLA Ops:
  7.2 81.1 %all-gather.4.cloned.1.call-start = ((), (), s32[]{:S(2)}) async-start(), calls=%async_computation | async-start | bytes 7569408 | tf_op jit(solution)/shard_map/all_gather | solution.py:16
  7.9 199.4 %all-gather.6.cloned.1.call-start = ((), (), s32[]{:S(2)}) async-start(), calls=%async_computation.1 | async-start | bytes 8704000 | tf_op jit(solution)/shard_map/all_gather | solution.py:24
  222.1 106.1 %copy-start = (s32[896]{0:T(1024)S(1)}, s32[896]{0:T(1024)}, u32[]{:S(2)}) copy-start(s32[896]{0:T(1024)} %param.9) | copy-start | bytes 10756
  222.1 227.4 %copy-start.3 = (s32[28]{0:T(128)S(1)}, s32[28]{0:T(128)}, u32[]{:S(2)}) copy-start(s32[28]{0:T(128)} %param.11) | copy-start | bytes 340
  222.1 228.0 %copy-start.2 = (s32[28]{0:T(128)S(1)}, s32[28]{0:T(128)}, u32[]{:S(2)}) copy-start(s32[28]{0:T(128)} %param.10) | copy-start | bytes 340
  450.0 103.0 %copy-start.1 = (f32[28]{0:T(128)}, f32[28]{0:T(128)S(1)}, u32[]{:S(2)}) copy-start(f32[28]{0:T(128)S(1)} %get-tuple-element.15) | copy-start | bytes 340
Sparse Core Ops, SparseCore 0:
  11.0 77.1 all-gather.3
  90.3 117.0 all-gather.5
where the time goes:
time: 561 us; the launch traced here: 560 us
  blocking collectives  321 us (57%)
  waiting for transfers between devices  170 us (30%)
  local copies, waits for them, and re-layouts  30.2 us (5%)
  matrix products  14.7 us (3%)
  between operations  14.1 us (3%)
  other arithmetic  9.96 us (2%)
    psum x1, blocking collectives, body(): lax.psum((total * scale, (spread + (top - best) * total) * scale, target_...  121 us
    all_gather x1, waiting for transfers between devices, body(): lax.all_gather(head_weight, 'dp', axis=0, tiled=True)  114 us
    psum x1, blocking collectives, body(): seq_sums, seq_live = lax.psum((seq_sums, seq_live), ('dp', 'tensor'))  102 us
    pmax x1, blocking collectives, body(): best = lax.pmax(top, 'tensor')  73.2 us
    all_gather x1, waiting for transfers between devices, body(): lax.all_gather(hidden, 'tensor', axis=1, tiled=True)  54 us
    gather x1, local copies, waits for them, and re-layouts, body(): jnp.take_along_axis(scores, jnp.clip(local_ids, 0, vocab_dev - 1)[:, None...  30.1 us
    all_gather x1, blocking collectives, body(): lax.all_gather(gain, 'tensor', axis=0, tiled=True)  24.1 us
    dot_general x1, matrix products, body(): jnp.dot(normed, lax.all_gather(head_weight, 'dp', axis=0, tiled=True), pr...  14.7 us
  transfers between devices with their start and end apart: 2, of which 2 were waited for; matrix products, arithmetic and copies ran while one was open for 1% of the time, Pallas kernels for 0%

commit v1 on v0

--- a/solution.py
+++ b/solution.py
@@ -13,7 +13,9 @@
     share = tok_rows // shards
     vocab_dev = head_weight.shape[1]
     whole, gains = (
-        lax.all_gather(hidden, "tensor", axis=1, tiled=True),
+        jnp.concatenate(
+            lax.all_to_all(jnp.stack([hidden] * lax.axis_size("tensor")), "tensor", 0, 0), axis=1
+        ),
         lax.all_gather(gain, "tensor", axis=0, tiled=True),
     )
     values = whole.astype(jnp.float32)

time: 561 us -> 509 us (0.907)
  waiting for transfers between devices: 170 us -> 0.69 us
  blocking collectives: 321 us -> 415 us
  starting transfers between devices: 0.08 us -> 11.5 us
  other arithmetic: 9.96 us -> 16.6 us
    all_gather x1, waiting for transfers between devices: 114 us -> 0.01 us  [body(): lax.all_gather(head_weight, 'dp', axis=0, tiled=True)]
    all_gather x1, blocking collectives: 24.1 us -> 119 us  [body(): lax.all_gather(gain, 'tensor', axis=0, tiled=True)]
    all_gather x1 -> x0, waiting for transfers between devices: 54 us -> none  [body(): lax.all_gather(hidden, 'tensor', axis=1, tiled=True)]
    all_to_all x0 -> x1, starting transfers between devices: none -> 11.5 us  [body(): lax.all_to_all(jnp.stack([hidden] * lax.axis_size('tensor')), 'tensor', 0...]
    pmax x1, blocking collectives: 73.2 us -> 62.2 us  [body(): best = lax.pmax(top, 'tensor')]
    convert_element_type x0 -> x1, other arithmetic: none -> 7.82 us  [body(): (values * lax.rsqrt(meansq + 1e-05) * gains.astype(jnp.float32)).astype(j...]
  transfers between devices with their start and end apart: 2 -> 2, of which waited for: 2 -> 0; matrix products, arithmetic and copies ran while one was open for 1% -> 4% of each run, Pallas kernels for 0% -> 0%
where the time goes in v1:
time: 509 us; the launch traced here: 507 us
  blocking collectives  415 us (82%)
  local copies, waits for them, and re-layouts  35.3 us (7%)
  other arithmetic  16.6 us (3%)
  matrix products  14.5 us (3%)
  between operations  14.2 us (3%)
  starting transfers between devices  11.5 us (2%)
    psum x1, blocking collectives, body(): lax.psum((total * scale, (spread + (top - best) * total) * scale, target_...  126 us
    all_gather x1, blocking collectives, body(): lax.all_gather(gain, 'tensor', axis=0, tiled=True)  119 us
    psum x1, blocking collectives, body(): seq_sums, seq_live = lax.psum((seq_sums, seq_live), ('dp', 'tensor'))  107 us
    pmax x1, blocking collectives, body(): best = lax.pmax(top, 'tensor')  62.2 us
    gather x1, local copies, waits for them, and re-layouts, body(): jnp.take_along_axis(scores, jnp.clip(local_ids, 0, vocab_dev - 1)[:, None...  30.1 us
    dot_general x1, matrix products, body(): jnp.dot(normed, lax.all_gather(head_weight, 'dp', axis=0, tiled=True), pr...  14.5 us
    all_to_all x1, starting transfers between devices, body(): lax.all_to_all(jnp.stack([hidden] * lax.axis_size('tensor')), 'tensor', 0...  11.5 us
  transfers between devices with their start and end apart: 2, of which 0 were waited for; matrix products, arithmetic and copies ran while one was open for 4% of the time, Pallas kernels for 0%

profile of v1, /device:TPU:1, one launch (start us, length us, event | category | flops | bytes accessed | tf_op | source)
XLA Modules:
  0.0 507.4 jit_solution(12041670304629532942)
XLA Ops:
  7.2 0.0 all-gather.3.cloned.1.call-start
  7.2 0.7 all-gather.3.cloned.1.call-update
  7.9 1.1 copy.11
  9.0 4.1 stack.2
  13.0 0.0 copy-start.2
  13.1 0.0 copy-start
  13.1 0.0 copy-start.4
  13.1 11.5 %all-to-all-start = ((bf16[32,896,128]{1,2,0:T(8,128)(2,1)}), bf16[32,896,128]{1,2,0:T(8,128)(2,1)}, u32[]{:S(2)}, u32[]{:S(2)}) async-start(bf16[32,896,128]{1,2,0:T(8,128)(2,1)} %stack.2), calls=%async_computation | async-start | bytes 14680064 | tf_op jit(solution)/shard_map/all_to_all | solution.py:17
  24.6 0.0 copy-done.2
  24.6 119.4 %all-gather = bf16[32,1,128]{2,1,0:T(2,128)(2,1)S(1)} all-gather(bf16[1,1,128]{2,1,0:T(2,128)(2,1)S(1)} %bitcast.15), channel_id=1, replica_groups=mesh['dp'=16,'tensor'=32] {'tensor'}, dimensions={0}, use_global_device_ids=true | all-gather | bytes 8448 | tf_op jit(solution)/shard_map/all_gather | solution.py:19
  144.0 0.0 copy-done
  144.0 0.0 copy-done.4
  144.1 0.0 all-to-all-done
  144.1 4.8 multiply_reduce_fusion
  148.9 7.8 %fusion.1 = bf16[896,4096]{0,1:T(8,128)(2,1)} fusion(f32[4096]{0:T(1024)S(1)} %bitcast.14, f32[896]{0:T(1024)S(1)} %add_rsqrt_fusion, bf16[32,896,128]{1,2,0:T(8,128)(2,1)} %all-to-all-done), kind=kLoop, calls=%fused_computation.3 | loop fusion | flops 14680064 | bytes 14700032 | tf_op jit(solution)/shard_map/convert_element_type | solution.py:23
  156.7 0.0 all-gather.3.cloned.1.call-done
  156.7 14.5 %fusion.7 = (f32[896]{0:T(1024)S(1)}, f32[896,1000]{0,1:T(8,128)}) fusion(bf16[896,4096]{0,1:T(8,128)(2,1)} %fusion.1, bf16[4096,1000]{0,1:T(8,128)(2,1)} %all-gather.3.cloned.1.call-done), kind=kOutput, calls=%fused_computation.26 | convolution fusion | flops 7340926976 | bytes 19119616 | tf_op jit(solution)/shard_map/dot_general | solution.py:24
  171.2 0.0 copy-start.3
  171.2 62.2 %pmax.7 = f32[896]{0:T(1024)S(1)} all-reduce(f32[896]{0:T(1024)S(1)} %get-tuple-element.16), channel_id=1, replica_groups=mesh['dp'=16,'tensor'=32] {'tensor'}, use_global_device_ids=true, to_apply=%region_3.0 | all-reduce | flops 896 | bytes 7168 | tf_op jit(solution)/shard_map/pmax | solution.py:41
  233.3 2.7 fusion.2
  236.1 30.1 %gather_fusion = f32[896]{0:T(1024)S(1)} fusion(f32[896,1000]{0,1:T(8,128)} %get-tuple-element.17, s32[896]{0:T(1024)S(1)} %fusion.6), kind=kCustom, calls=%fused_computation | custom fusion | bytes 14336 | tf_op jit(solution)/shard_map/jit(take_along_axis)/gather | solution.py:36
  266.3 125.6 %all-reduce.1 = (f32[896]{0:T(1024)S(1)}, f32[896]{0:T(1024)S(1)}, f32[896]{0:T(1024)S(1)}) all-reduce(f32[896]{0:T(1024)S(1)} %select_select_fusion, f32[896]{0:T(1024)S(1)} %get-tuple-element.13, f32[896]{0:T(1024)S(1)} %get-tuple-element.12), channel_id=1, replica_groups=mesh['dp'=16,'tensor'=32] {'tensor'}, use_global_device_ids=true, to_apply=%region_1.0 | all-reduce | flops 2688 | bytes 21504 | tf_op jit(solution)/shard_map/psum | solution.py:43
  391.9 0.6 subtract_multiply_fusion
  392.4 0.0 copy-start.1
  392.5 0.0 copy-done.3
  392.5 0.1 select_reduce_fusion
  392.6 107.4 %all-reduce = (f32[64]{0:T(128)S(1)}, f32[64]{0:T(128)S(1)}) all-reduce(f32[64]{0:T(128)S(1)} %get-tuple-element.6, f32[64]{0:T(128)S(1)} %get-tuple-element.5), channel_id=1, replica_groups=mesh['dp'=16,'tensor'=32] {'dp','tensor'}, use_global_device_ids=true, to_apply=%region_9.10 | all-reduce | flops 128 | bytes 1024 | tf_op jit(solution)/shard_map/psum | solution.py:58
  500.0 0.5 maximum_divide_fusion
  500.5 0.0 copy-done.1
  (10 shorter events, 0.1 us)
Async XLA Ops:
  7.2 149.5 %all-gather.3.cloned.1.call-start = ((), (), s32[]{:S(2)}) async-start(), calls=%async_computation.1 | async-start | bytes 8704000 | tf_op jit(solution)/shard_map/all_gather | solution.py:26
  13.0 11.5 %copy-start.2 = (bf16[128]{0:T(256)(128)(2,1)S(1)}, bf16[128]{0:T(256)(128)(2,1)}, u32[]{:S(2)}) copy-start(bf16[128]{0:T(256)(128)(2,1)} %param.7) | copy-start | bytes 772
  13.1 130.9 %copy-start = (s32[896]{0:T(1024)S(1)}, s32[896]{0:T(1024)}, u32[]{:S(2)}) copy-start(s32[896]{0:T(1024)} %param.9) | copy-start | bytes 10756
  13.1 131.0 %copy-start.4 = (s32[28]{0:T(128)S(1)}, s32[28]{0:T(128)}, u32[]{:S(2)}) copy-start(s32[28]{0:T(128)} %param.11) | copy-start | bytes 340
  13.1 131.0 %all-to-all-start = ((bf16[32,896,128]{1,2,0:T(8,128)(2,1)}), bf16[32,896,128]{1,2,0:T(8,128)(2,1)}, u32[]{:S(2)}, u32[]{:S(2)}) async-start(bf16[32,896,128]{1,2,0:T(8,128)(2,1)} %stack.2), calls=%async_computation | async-start | bytes 14680064 | tf_op jit(solution)/shard_map/all_to_all | solution.py:17
  171.2 221.3 %copy-start.3 = (s32[28]{0:T(128)S(1)}, s32[28]{0:T(128)}, u32[]{:S(2)}) copy-start(s32[28]{0:T(128)} %param.10) | copy-start | bytes 340
  392.4 108.1 %copy-start.1 = (f32[28]{0:T(128)}, f32[28]{0:T(128)S(1)}, u32[]{:S(2)}) copy-start(f32[28]{0:T(128)S(1)} %get-tuple-element.15) | copy-start | bytes 340
Sparse Core Ops, SparseCore 0:
  10.0 121.7 all-gather.2
